TPU v7x, 256 devices: a whole 4x4x8 slice. The times are simulated.
256 devices in a mesh: leaf: 32 (over z, y), front: 8 (over x, core).
Axes of the slice: x: 4, y: 4, z: 8, core: 2. Of those that a mesh axis runs over, the one named last changes fastest.
Arguments:
- leaf_fronts: float32 [32, 1, 2048, 2048], P('leaf', None, 'front'), may hold values from -40 to 40, as said below
- screen_weights: float32 [32, 1, 2048], P('leaf', None, 'front'), may hold values from 0.1 to 2
- parent_tile_index: int32 [32, 1, 12], replicated, may hold values from 0 to 31, as said below
Outputs:
- leaf_panel: float32 [32, 1, 2048, 512], P('leaf', None, 'front')
- parent_panel: float32 [32, 1, 2048, 128], P('leaf', None, 'front')
- parent_update: float32 [32, 1, 2048, 3968], P('leaf', None, 'front')
Inputs may be any that keep to these rules, and one draw needn't show every extreme that they name: `leaf_fronts`: each first-level front is symmetric positive definite. `parent_tile_index`: entry [i, g, a] is the tile of parent (i // 2, g) that receives contribution tile t = 4 * (a // 3) + a % 3 + 1 of front (i, g); tile p covers rows p * 128 to (p + 1) * 128 - 1. The entries of one front are distinct, tile 1 always goes to parent tile 0, and p * 128 // 512 == t * 128 // 256.
All inputs are finite; a program needn't handle non-finite values.
Results may differ from a plain program's by a relative error of at most 0.00013.
Values sent between devices are 32-bit elements; how exact they have to be, the bound alone decides.
A program may use at most 128 MiB of HBM per device.

v0:
```python
import functools

import jax
import jax.numpy as jnp
from jax import lax
from jax.experimental import pallas as pl
from jax.experimental.pallas import tpu as pltpu
from jax.sharding import PartitionSpec as P

MESH = pl.DeviceIdType.MESH
HIGHEST = lax.Precision.HIGHEST
NT = (((1,), (1,)), ((), ()))
NN = (((1,), (0,)), ((), ()))
TN = (((0,), (0,)), ((), ()))
TILE = 128
SEP2_TILES = 8
f32 = jnp.float32
bf16 = jnp.bfloat16


def exact_dot(a, b, dims):
    return lax.dot_general(a, b, dims, precision=HIGHEST, preferred_element_type=f32)


def thirds(x):
    high = x.astype(bf16)
    rest = x - high.astype(f32)
    mid = rest.astype(bf16)
    low = (rest - mid.astype(f32)).astype(bf16)
    return high, mid, low


def halves(x):
    high = x.astype(bf16)
    return high, (x - high.astype(f32)).astype(bf16)


def left_stack(high, low):
    return jnp.concatenate([high, low, high], axis=1)


def right_stack(high, low):
    return jnp.concatenate([high, high, low], axis=1)


def stack_dot(left, right):
    return lax.dot_general(left, right, NT, preferred_element_type=f32)


def start_block(block, mat, tile, upper):
    row = lax.broadcasted_iota(jnp.int32, (TILE, TILE), 0)
    col = lax.broadcasted_iota(jnp.int32, (TILE, TILE), 1)
    mat[:, :TILE] = block
    mat[:, TILE:] = (row == col).astype(f32)
    tile[...] = mat[0:8, :]
    upper[...] = jnp.zeros_like(upper)


def twice(x):
    return jnp.concatenate([x, x], axis=1)


def factor_panel(step, mat, tile, upper, inv):
    base = step * 8
    sub = lax.broadcasted_iota(jnp.int32, (8, TILE), 0)
    sub_wide = lax.broadcasted_iota(jnp.int32, (8, 2 * TILE), 0)
    high, mid, low = thirds(upper[...])
    left = jnp.concatenate([high, high, mid, high, low, mid], axis=0)[:, :TILE]
    right = jnp.concatenate([high, mid, high, low, high, mid], axis=0)
    mat[...] -= lax.dot_general(left, right, TN, preferred_element_type=f32)
    rows = tile[...]
    entry = {}
    for j in range(8):
        picked = jnp.take_along_axis(rows[:, :TILE], jnp.full((8, TILE), base + j, jnp.int32), axis=1)
        for i in range(j, 8):
            entry[i, j] = jnp.broadcast_to(picked[i : i + 1, :], (8, TILE))
    done = []
    packed = jnp.zeros((8, 2 * TILE), f32)
    for j in range(8):
        pivot = entry[j, j]
        scale = lax.rsqrt(pivot)
        scale = scale * (1.5 - 0.5 * pivot * scale * scale)
        for i in range(j + 1, 8):
            entry[i, j] = entry[i, j] * scale
        for i in range(j + 1, 8):
            for k in range(j + 1, i + 1):
                entry[i, k] = entry[i, k] - entry[i, j] * entry[k, j]
        row = jnp.broadcast_to(rows[j : j + 1, :], (8, 2 * TILE))
        for p in range(j):
            row = row - twice(entry[j, p]) * done[p]
        row = row * twice(scale)
        done.append(row)
        packed = jnp.where(sub_wide == j, row, packed)
    upper[...] = packed
    inv[pl.ds(pl.multiple_of(base, 8), 8), :] = packed[:, TILE:]
    after = pl.multiple_of(jnp.minimum(base + 8, TILE - 8), 8)
    total = mat[pl.ds(after, 8), :]
    for p in range(8):
        weight = jnp.take_along_axis(done[p][:, :TILE], after + sub, axis=1)
        total = total - twice(weight) * done[p]
    tile[...] = total


def exchange_kernel(front, weights, gathered, sibling_rows, weight_rows, local_sem, send_sem, recv_sem, row_send, row_recv):
    leaf = lax.axis_index("leaf")
    front_id = lax.axis_index("front")
    half = lax.rem(leaf, 2)
    chip = lax.div(front_id, 2)
    core = lax.rem(front_id, 2)
    chips = lax.div(lax.axis_size("front"), 2)

    def chip_at(offset):
        return lax.rem(chip + offset + chips, chips)

    sibling = (leaf + 1 - 2 * half, front_id)
    right = (leaf, chip_at(1) * 2 + core)
    left = (leaf, chip_at(-1) * 2 + core)
    partner = (leaf, front_id + 1 - 2 * core)
    everyone = (sibling, right, left, partner)

    weight_rows[0:1, :] = weights[0:1, 0:TILE]
    weight_rows[1:2, :] = weights[0:1, TILE : 2 * TILE]
    weight_rows[2:8, :] = jnp.zeros((6, TILE), f32)
    staged = []

    def stage(src, dst):
        copy = pltpu.make_async_copy(src, dst, local_sem.at[len(staged)])
        copy.start()
        staged.append(copy)

    for r in range(2):
        slot = gathered.at[half, 2 * front_id + r]
        rows = pl.ds(r * TILE, TILE)
        for k in range(4):
            stage(front.at[rows, pl.ds(4 * k * TILE, TILE)], slot.at[:, pl.ds(k * TILE, TILE)])
        stage(front.at[pl.ds(r * TILE + 8, TILE - 8), pl.ds(TILE, TILE)], slot.at[pl.ds(8, TILE - 8), pl.ds(4 * TILE, TILE)])
        head = slot.at[pl.ds(0, 8), pl.ds(4 * TILE, TILE)]
        if r == 1:
            stage(front.at[pl.ds(TILE, 8), pl.ds(TILE, TILE)], head)
        else:
            number = len(staged)

            @pl.when(core == 1)
            def _():
                pltpu.make_async_copy(front.at[pl.ds(0, 8), pl.ds(TILE, TILE)], head, local_sem.at[number]).start()

            @pl.when(core == 0)
            def _():
                pltpu.make_async_copy(weight_rows, head, local_sem.at[number]).start()

            staged.append(pltpu.make_async_copy(weight_rows, head, local_sem.at[number]))

    barrier = pltpu.get_barrier_semaphore()
    for device in everyone:
        pl.semaphore_signal(barrier, inc=1, device_id=device, device_id_type=MESH)
    pl.semaphore_wait(barrier, 4)
    for copy in staged:
        copy.wait()

    sends = []

    def slot_of(child, offset, r, other=False):
        c = 1 - core if other else core
        return child, chip_at(offset) * 4 + c * 2 + r

    def send(where, device):
        child, t = where
        copy = pltpu.make_async_remote_copy(
            src_ref=gathered.at[child, t],
            dst_ref=gathered.at[child, t],
            send_sem=send_sem.at[len(sends)],
            recv_sem=recv_sem.at[child, t],
            device_id=device,
            device_id_type=MESH,
        )
        copy.start()
        sends.append(copy)

    def arrive(where):
        child, t = where
        pltpu.make_async_remote_copy(
            src_ref=gathered.at[child, t],
            dst_ref=gathered.at[child, t],
            send_sem=send_sem.at[0],
            recv_sem=recv_sem.at[child, t],
            device_id=partner,
            device_id_type=MESH,
        ).wait_recv()

    own, other = half, 1 - half
    for r in range(2):
        for device in everyone:
            send(slot_of(own, 0, r), device)

    def row_copy(r, g):
        return pltpu.make_async_remote_copy(
            src_ref=front.at[pl.ds(r * TILE, TILE), pl.ds((4 * g + 1) * TILE, 3 * TILE)],
            dst_ref=sibling_rows.at[pl.ds(r * TILE, TILE), pl.ds(3 * g * TILE, 3 * TILE)],
            send_sem=row_send.at[r, g],
            recv_sem=row_recv.at[r, g],
            device_id=sibling,
            device_id_type=MESH,
        )

    def forward(child, offset, r, *devices):
        where = slot_of(child, offset, r)
        arrive(where)
        for device in devices:
            send(where, device)

    forward(own, -1, 0, right, partner)
    forward(own, 1, 0, partner)
    forward(other, 0, 0, right, left, partner)
    forward(other, 0, 1, right, left, partner)
    for g in range(4):
        row_copy(1, g).start()

    @pl.when(core == 1)
    def _():
        for g in range(4):
            row_copy(0, g).start()

    forward(own, 1, 1, left, partner)
    forward(own, -1, 1, partner)
    forward(other, -1, 0, right, partner)
    forward(other, 1, 0, partner)
    forward(other, 1, 1, left, partner)
    forward(other, -1, 1, partner)
    forward(own, 2, 0, partner)
    forward(own, 2, 1, partner)
    forward(other, 2, 0, partner)
    forward(other, 2, 1, partner)
    for child in (own, other):
        for offset in (0, -1, 1, 2):
            for r in range(2):
                arrive(slot_of(child, offset, r, True))
    for copy in sends:
        copy.wait_send()
    for g in range(4):
        row_copy(1, g).wait()

    @pl.when(core == 1)
    def _():
        for g in range(4):
            row_copy(0, g).wait()


def exchange(front, weights):
    rows, width = front.shape
    tiles = width // TILE
    return pl.pallas_call(
        exchange_kernel,
        out_shape=(
            jax.ShapeDtypeStruct((2, tiles, TILE, 5 * TILE), f32),
            jax.ShapeDtypeStruct((rows, 12 * TILE), f32),
        ),
        in_specs=[pl.BlockSpec(memory_space=pl.ANY), pl.BlockSpec(memory_space=pltpu.VMEM)],
        out_specs=(pl.BlockSpec(memory_space=pl.ANY), pl.BlockSpec(memory_space=pl.ANY)),
        scratch_shapes=[
            pltpu.VMEM((8, TILE), f32),
            pltpu.SemaphoreType.DMA((12,)),
            pltpu.SemaphoreType.DMA((30,)),
            pltpu.SemaphoreType.DMA((2, tiles)),
            pltpu.SemaphoreType.DMA((2, 4)),
            pltpu.SemaphoreType.DMA((2, 4)),
        ],
        compiler_params=pltpu.CompilerParams(collective_id=0, has_side_effects=True),
        name="exchange",
    )(front, weights)


def corner_kernel(gathered, factors, corner, inv, mat, tile, upper, sem):
    copies = []
    for child in range(2):
        for k in range(4):
            copy = pltpu.make_async_copy(
                gathered.at[child, 4 * k, :, pl.ds(0, 4 * TILE)],
                corner.at[child, pl.ds(k * TILE, TILE), :],
                sem.at[child, k],
            )
            copy.start()
            copies.append(copy)
    for copy in copies:
        copy.wait()
    for k in range(4):
        here = slice(k * TILE, (k + 1) * TILE)
        for child in range(2):
            start_block(corner[child, here, here], mat.at[child], tile.at[child], upper.at[child])

        @pl.loop(0, TILE // 8)
        def _(step):
            for child in range(2):
                factor_panel(step, mat.at[child], tile.at[child], upper.at[child], inv.at[child])

        for child in range(2):
            finish_block(k, corner.at[child], inv.at[child], factors.at[child])


def finish_block(k, corner, inv, factors):
    here = slice(k * TILE, (k + 1) * TILE)
    inverse = inv[...]
    level, place = divmod(k, 2)
    if place == 0:
        factors[level, 0:TILE, 0:TILE] = inverse
        factors[level, 0:TILE, TILE:] = jnp.zeros((TILE, TILE), f32)
    else:
        before = slice((k - 1) * TILE, k * TILE)
        middle = exact_dot(corner[here, before], factors[level, 0:TILE, 0:TILE], NN)
        factors[level, TILE:, 0:TILE] = -exact_dot(inverse, middle, NN)
        factors[level, TILE:, TILE:] = inverse
    if k < 3:
        rest = slice((k + 1) * TILE, 4 * TILE)
        below = exact_dot(corner[rest, here], inverse, NT)
        corner[rest, here] = below
        corner[rest, rest] -= exact_dot(below, below, NT)
        if level == 0:
            cut = (1 - place) * TILE
            factors[2, :, place * TILE : (place + 1) * TILE] = below[cut:, :]


def factor_corners(gathered):
    return pl.pallas_call(
        corner_kernel,
        out_shape=jax.ShapeDtypeStruct((2, 3, 2 * TILE, 2 * TILE), f32),
        in_specs=[pl.BlockSpec(memory_space=pl.ANY)],
        out_specs=pl.BlockSpec(memory_space=pltpu.VMEM),
        scratch_shapes=[
            pltpu.VMEM((2, 4 * TILE, 4 * TILE), f32),
            pltpu.VMEM((2, TILE, TILE), f32),
            pltpu.VMEM((2, TILE, 2 * TILE), f32),
            pltpu.VMEM((2, 8, 2 * TILE), f32),
            pltpu.VMEM((2, 8, 2 * TILE), f32),
            pltpu.SemaphoreType.DMA((2, 4)),
        ],
        compiler_params=pltpu.CompilerParams(vmem_limit_bytes=40 * 2**20),
        name="corners",
    )(gathered)


def assemble_kernel(
    index, gathered, front, sibling_rows, factors, weights,
    leaf_panel, parent_panel, parent_update,
    chunk, own_front, sib_front, weight_rows, solver, high, low, column, parent, parent_high, parent_low,
    inv, mat, tile, upper, child_of, sem, row_sem,
):
    leaf = lax.axis_index("leaf")
    front_id = lax.axis_index("front")
    half = lax.rem(leaf, 2)
    first = leaf - half

    loads = {}
    for g in range(4):
        for child in range(2):
            loads[child, g] = pltpu.make_async_copy(
                gathered.at[child, pl.ds(4 * g + 1, 3)], chunk.at[child, g], sem.at[child, g]
            )
            loads[child, g].start()
    row_loads = [
        pltpu.make_async_copy(front, own_front, row_sem.at[0]),
        pltpu.make_async_copy(sibling_rows, sib_front, row_sem.at[1]),
        pltpu.make_async_copy(gathered.at[0, 0, pl.ds(0, 8), pl.ds(4 * TILE, TILE)], weight_rows, row_sem.at[2]),
    ]
    for copy in row_loads:
        copy.start()

    @pl.loop(0, 32)
    def _(p):
        child_of[0, p] = -1
        child_of[1, p] = -1

    for child in range(2):
        for a in range(12):
            child_of[child, index[first + child, a]] = a

    for child in range(2):
        for j in range(3):
            solver[child, j] = right_stack(*halves(factors[child, j]))

    def solve(child, columns):
        one = stack_dot(left_stack(*halves(columns[:, : 2 * TILE])), solver[child, 0])
        one_high, one_low = halves(one)
        two = columns[:, 2 * TILE :] - stack_dot(left_stack(one_high, one_low), solver[child, 2])
        two = stack_dot(left_stack(*halves(two)), solver[child, 1])
        return one, two

    for g in range(4):
        for child in range(2):
            loads[child, g].wait()
            block = chunk[child, g].reshape(3 * TILE, 5 * TILE)
            one, two = solve(child, block[:, : 4 * TILE])
            whole_high, whole_low = halves(jnp.concatenate([one, two], axis=1))
            high[child, pl.ds(3 * g, 3)] = whole_high.reshape(3, TILE, 4 * TILE)
            low[child, pl.ds(3 * g, 3)] = whole_low.reshape(3, TILE, 4 * TILE)
            product = stack_dot(left_stack(whole_high, whole_low), right_stack(high[child, 0], low[child, 0]))
            column[child, pl.ds(3 * g, 3)] = (block[:, 4 * TILE :] - product).reshape(3, TILE, TILE)

    for copy in row_loads:
        copy.wait()
    own_columns = jnp.concatenate([own_front[:, 4 * k * TILE : (4 * k + 1) * TILE] for k in range(4)], axis=1)
    one, two = solve(half, own_columns)
    leaf_panel[:, : 2 * TILE] = one
    leaf_panel[:, 2 * TILE :] = two

    row = lax.broadcasted_iota(jnp.int32, (TILE, TILE), 0)
    col = lax.broadcasted_iota(jnp.int32, (TILE, TILE), 1)
    near = jnp.where(jnp.abs(row - col) == 1, 1.0, 0.0)
    above = jnp.where((row == 0) & (col == TILE - 1), 1.0, 0.0)
    under = jnp.where((row == TILE - 1) & (col == 0), 1.0, 0.0)

    @pl.loop(0, 32)
    def _(p):
        total = jnp.zeros((TILE, TILE), f32)
        for child in range(2):
            a = child_of[child, p]
            total = total + jnp.where(a >= 0, column[child, jnp.maximum(a, 0)], 0.0)
        parent[p] = total

    parent[0] += jnp.where(row == col, weight_rows[0:1, :] + 4.0, 0.0) - near
    parent[1] -= above

    start_block(parent[0], mat, tile, upper)

    @pl.loop(0, TILE // 8)
    def _(step):
        factor_panel(step, mat, tile, upper, inv)

    last = right_stack(*halves(inv[...]))
    for q in range(8):
        block = parent[4 * q : 4 * q + 4].reshape(4 * TILE, TILE)
        done = stack_dot(left_stack(*halves(block)), last)
        parent[4 * q : 4 * q + 4] = done.reshape(4, TILE, TILE)
        done_high, done_low = halves(done)
        parent_high[4 * q * TILE : 4 * (q + 1) * TILE, :] = done_high
        parent_low[4 * q * TILE : 4 * (q + 1) * TILE, :] = done_low

    place = 4 * front_id + 2 * half
    parent_panel[...] = parent[pl.ds(place, 2)].reshape(2 * TILE, TILE)
    here = pl.ds(pl.multiple_of(place * TILE, TILE), 2 * TILE)
    mine = left_stack(parent_high[here, :], parent_low[here, :])
    for start in range(TILE, 32 * TILE, 4 * TILE):
        stop = min(start + 4 * TILE, 32 * TILE)
        there = right_stack(parent_high[start:stop, :], parent_low[start:stop, :])
        parent_update[:, start - TILE : stop - TILE] = -stack_dot(mine, there)

    def columns_of(p):
        return pl.ds(pl.multiple_of((p - 1) * TILE, TILE), TILE)

    for kin in range(2):
        child = half if kin == 0 else 1 - half
        source = own_front if kin == 0 else sib_front
        for r in range(2):
            a = child_of[child, place + r]
            rows = pl.ds(r * TILE, TILE)

            @pl.when(a >= 0)
            def _():
                local = 4 * lax.div(a, 3) + lax.rem(a, 3) + 1 - 2 * front_id
                source_rows = pl.ds(pl.multiple_of(local * TILE, TILE), TILE)
                lead = left_stack(high[child, a], low[child, a])
                for g in range(4):
                    others = right_stack(
                        high[child, pl.ds(3 * g, 3)].reshape(3 * TILE, 4 * TILE),
                        low[child, pl.ds(3 * g, 3)].reshape(3 * TILE, 4 * TILE),
                    )
                    product = stack_dot(lead, others)
                    for m in range(3):
                        b = 3 * g + m
                        p = index[first + child, b]
                        t = 4 * g + m + 1 if kin == 0 else b
                        value = source[source_rows, t * TILE : (t + 1) * TILE] - product[:, m * TILE : (m + 1) * TILE]
                        if b == 0:
                            continue
                        parent_update[rows, columns_of(p)] += value

    for r in range(2):
        p = place + r
        rows = slice(r * TILE, (r + 1) * TILE)
        own_weights = weights[0:1, r * TILE : (r + 1) * TILE]
        inside = p < SEP2_TILES

        @pl.when(p >= 1)
        def _():
            extra = jnp.where(inside, 1.0, 0.0)
            parent_update[rows, columns_of(p)] += jnp.where(row == col, own_weights + 4.0 * extra, 0.0) - near * extra

        @pl.when((p >= 2) & inside)
        def _():
            parent_update[rows, columns_of(p - 1)] -= above

        @pl.when(p + 1 < SEP2_TILES)
        def _():
            parent_update[rows, columns_of(p + 1)] -= under


def assemble(index, gathered, front, sibling_rows, factors, weights):
    rows, width = front.shape
    anywhere = pl.BlockSpec(memory_space=pl.ANY)
    local = pl.BlockSpec(memory_space=pltpu.VMEM)
    return pl.pallas_call(
        assemble_kernel,
        out_shape=(
            jax.ShapeDtypeStruct((rows, 4 * TILE), f32),
            jax.ShapeDtypeStruct((rows, TILE), f32),
            jax.ShapeDtypeStruct((rows, 31 * TILE), f32),
        ),
        in_specs=[pl.BlockSpec(memory_space=pltpu.SMEM), anywhere, anywhere, anywhere, local, local],
        out_specs=(local, local, local),
        scratch_shapes=[
            pltpu.VMEM((2, 4, 3, TILE, 5 * TILE), f32),
            pltpu.VMEM((rows, width), f32),
            pltpu.VMEM((rows, 12 * TILE), f32),
            pltpu.VMEM((8, TILE), f32),
            pltpu.VMEM((2, 3, 2 * TILE, 6 * TILE), bf16),
            pltpu.VMEM((2, 12, TILE, 4 * TILE), bf16),
            pltpu.VMEM((2, 12, TILE, 4 * TILE), bf16),
            pltpu.VMEM((2, 12, TILE, TILE), f32),
            pltpu.VMEM((32, TILE, TILE), f32),
            pltpu.VMEM((32 * TILE, TILE), bf16),
            pltpu.VMEM((32 * TILE, TILE), bf16),
            pltpu.VMEM((TILE, TILE), f32),
            pltpu.VMEM((TILE, 2 * TILE), f32),
            pltpu.VMEM((8, 2 * TILE), f32),
            pltpu.VMEM((8, 2 * TILE), f32),
            pltpu.SMEM((2, 32), jnp.int32),
            pltpu.SemaphoreType.DMA((2, 4)),
            pltpu.SemaphoreType.DMA((3,)),
        ],
        compiler_params=pltpu.CompilerParams(vmem_limit_bytes=56 * 2**20),
        name="assemble",
    )(index, gathered, front, sibling_rows, factors, weights)


def on_device(leaf_fronts, screen_weights, parent_tile_index):
    front = leaf_fronts[0, 0]
    weights = screen_weights[0]
    index = parent_tile_index[:, 0]
    gathered, sibling_rows = exchange(front, weights)
    factors = factor_corners(gathered)
    leaf_panel, parent_panel, parent_update = assemble(index, gathered, front, sibling_rows, factors, weights)
    return leaf_panel[None, None], parent_panel[None, None], parent_update[None, None]


def solution(mesh):
    rows = P("leaf", None, "front", None)
    return jax.shard_map(
        on_device,
        mesh=mesh,
        in_specs=(rows, P("leaf", None, "front"), P()),
        out_specs=(rows, rows, rows),
        check_vma=False,
    )
```

profile of v0, /device:TPU:160, one launch (start us, length us, event | category | flops | bytes accessed | tf_op | source)
XLA Modules:
  0.0 131.6 jit_solution(14424470371254214885)
XLA Ops:
  0.6 1.4 %copy.6 = s32[32,1,12]{2,0,1:T(8,128)} copy(s32[32,1,12]{0,1,2:T(1,128)} %param.5) | data formatting | bytes 3072 | tf_op args[2]
  2.0 70.4 %exchange.1 = (f32[2,16,128,640]{3,2,1,0:T(8,128)}, f32[256,1536]{1,0:T(8,128)}) custom-call(f32[256,2048]{1,0:T(8,128)} %bitcast.6, f32[1,256]{1,0:T(1,128)} %bitcast.9), custom_call_target="tpu_custom_call" | custom-call | tf_op jit(solution)/shard_map/exchange/pallas_call | solution.py:251
  72.4 0.0 copy-start
  72.5 4.0 %copy-done = f32[2,16,128,640]{3,2,1,0:T(8,128)S(1)} copy-done((f32[2,16,128,640]{3,2,1,0:T(8,128)S(1)}, f32[2,16,128,640]{3,2,1,0:T(8,128)}, u32[]{:S(2)}) %copy-start) | copy-done | bytes 10485784
  76.4 24.4 %corners.1.factors = f32[2,3,256,256]{3,2,1,0:T(8,128)S(1)} custom-call(f32[2,16,128,640]{3,2,1,0:T(8,128)S(1)} %copy-done), custom_call_target="tpu_custom_call" | custom-call | tf_op jit(solution)/shard_map/corners/pallas_call | solution.py:322
  100.8 0.0 copy-start.1
  100.8 1.2 copy-done.1
  102.0 29.4 %assemble.1 = (f32[256,512]{1,0:T(8,128)}, f32[256,128]{1,0:T(8,128)}, f32[256,3968]{1,0:T(8,128)}) custom-call(s32[32,12]{1,0:T(8,128)} %bitcast.8, f32[2,16,128,640]{3,2,1,0:T(8,128)} %get-tuple-element.8.gathered, f32[256,2048]{1,0:T(8,128)} %bitcast.7, f32[256,1536]{1,0:T(8,128)} %get-tuple-element.9.sibling_rows, f32[2,3,256,256]{3,2,1,0:T(8,128)} %copy-done.1, ...), custom_call_target="tpu_custom_call" | custom-call | tf_op jit(solution)/shard_map/assemble/pallas_call | solution.py:499
Async XLA Ops:
  72.4 4.0 %copy-start = (f32[2,16,128,640]{3,2,1,0:T(8,128)S(1)}, f32[2,16,128,640]{3,2,1,0:T(8,128)}, u32[]{:S(2)}) copy-start(f32[2,16,128,640]{3,2,1,0:T(8,128)} %get-tuple-element.8.gathered) | copy-start | bytes 31457284
  100.8 1.2 copy-start.1
where the time goes:
time: 134 us; the launch traced here: 132 us
  Pallas kernels  124 us (93%)
  local copies, waits for them, and re-layouts  6.55 us (5%)
    pallas_call x1, Pallas kernels, exchange(): pl.pallas_call(exchange_kernel, out_shape=(jax.ShapeDtypeStruct((2, tiles...  70.4 us
    pallas_call x1, Pallas kernels, assemble(): pl.pallas_call(assemble_kernel, out_shape=(jax.ShapeDtypeStruct((rows, 4...  29.4 us
    pallas_call x1, Pallas kernels, factor_corners(): pl.pallas_call(corner_kernel, out_shape=jax.ShapeDtypeStruct((2, 3, 2 * T...  24.4 us
    unnamed x5, local copies, waits for them, and re-layouts  6.55 us

commit v1 on v0

v1 whole, which is shorter than its diff:
```python
import functools

import jax
import jax.numpy as jnp
from jax import lax
from jax.experimental import pallas as pl
from jax.experimental.pallas import tpu as pltpu
from jax.sharding import PartitionSpec as P

MESH = pl.DeviceIdType.MESH
HIGHEST = lax.Precision.HIGHEST
NT = (((1,), (1,)), ((), ()))
NN = (((1,), (0,)), ((), ()))
TN = (((0,), (0,)), ((), ()))
TILE = 128
SEP2_TILES = 8
f32 = jnp.float32
bf16 = jnp.bfloat16


def exact_dot(a, b, dims):
    return lax.dot_general(a, b, dims, precision=HIGHEST, preferred_element_type=f32)


def thirds(x):
    high = x.astype(bf16)
    rest = x - high.astype(f32)
    mid = rest.astype(bf16)
    low = (rest - mid.astype(f32)).astype(bf16)
    return high, mid, low


def halves(x):
    high = x.astype(bf16)
    return high, (x - high.astype(f32)).astype(bf16)


def left_stack(high, low):
    return jnp.concatenate([high, low, high], axis=1)


def right_stack(high, low):
    return jnp.concatenate([high, high, low], axis=1)


def stack_dot(left, right):
    return lax.dot_general(left, right, NT, preferred_element_type=f32)


def start_block(block, mat, tile, upper):
    row = lax.broadcasted_iota(jnp.int32, (TILE, TILE), 0)
    col = lax.broadcasted_iota(jnp.int32, (TILE, TILE), 1)
    mat[:, :TILE] = block
    mat[:, TILE:] = (row == col).astype(f32)
    tile[...] = mat[0:8, :]
    upper[...] = jnp.zeros_like(upper)


def twice(x):
    return jnp.concatenate([x, x], axis=1)


def factor_panel(step, mat, tile, upper, inv):
    base = step * 8
    sub = lax.broadcasted_iota(jnp.int32, (8, TILE), 0)
    sub_wide = lax.broadcasted_iota(jnp.int32, (8, 2 * TILE), 0)
    high, mid, low = thirds(upper[...])
    left = jnp.concatenate([high, high, mid, high, low, mid], axis=0)[:, :TILE]
    right = jnp.concatenate([high, mid, high, low, high, mid], axis=0)
    mat[...] -= lax.dot_general(left, right, TN, preferred_element_type=f32)
    rows = tile[...]
    entry = {}
    for j in range(8):
        picked = jnp.take_along_axis(rows[:, :TILE], jnp.full((8, TILE), base + j, jnp.int32), axis=1)
        for i in range(j, 8):
            entry[i, j] = jnp.broadcast_to(picked[i : i + 1, :], (8, TILE))
    done = []
    packed = jnp.zeros((8, 2 * TILE), f32)
    for j in range(8):
        pivot = entry[j, j]
        scale = lax.rsqrt(pivot)
        scale = scale * (1.5 - 0.5 * pivot * scale * scale)
        for i in range(j + 1, 8):
            entry[i, j] = entry[i, j] * scale
        for i in range(j + 1, 8):
            for k in range(j + 1, i + 1):
                entry[i, k] = entry[i, k] - entry[i, j] * entry[k, j]
        row = jnp.broadcast_to(rows[j : j + 1, :], (8, 2 * TILE))
        for p in range(j):
            row = row - twice(entry[j, p]) * done[p]
        row = row * twice(scale)
        done.append(row)
        packed = jnp.where(sub_wide == j, row, packed)
    upper[...] = packed
    inv[pl.ds(pl.multiple_of(base, 8), 8), :] = packed[:, TILE:]
    after = pl.multiple_of(jnp.minimum(base + 8, TILE - 8), 8)
    total = mat[pl.ds(after, 8), :]
    for p in range(8):
        weight = jnp.take_along_axis(done[p][:, :TILE], after + sub, axis=1)
        total = total - twice(weight) * done[p]
    tile[...] = total


def gather_factor_kernel(
    front, weights,
    sibling_rows, high, low, column, top, top_inv, own_panel,
    gathered, corner_in, corner, own_rows, factors, solver, lead, inv, mat, tile, upper,
    local_sem, first_send, first_recv, bulk_send, bulk_recv, row_send, row_recv,
):
    leaf = lax.axis_index("leaf")
    front_id = lax.axis_index("front")
    half = lax.rem(leaf, 2)
    chip = lax.div(front_id, 2)
    core = lax.rem(front_id, 2)
    chips = lax.div(lax.axis_size("front"), 2)
    own, other = half, 1 - half

    def chip_at(offset):
        return lax.rem(chip + offset + chips, chips)

    sibling = (leaf + 1 - 2 * half, front_id)
    right = (leaf, chip_at(1) * 2 + core)
    left = (leaf, chip_at(-1) * 2 + core)
    partner = (leaf, front_id + 1 - 2 * core)

    staged = []

    def stage(src, dst, condition=None):
        copy = pltpu.make_async_copy(src, dst, local_sem.at[len(staged)])
        staged.append((condition, copy))
        when(condition, copy.start)

    def when(condition, action):
        if condition is None:
            action()
        else:
            pl.when(condition)(lambda: action())

    def stage_row(r, slot, condition=None):
        rows = pl.ds(r * TILE, TILE)
        for k in range(4):
            stage(front.at[rows, pl.ds(4 * k * TILE, TILE)], slot.at[:, pl.ds(k * TILE, TILE)], condition)
        stage(front.at[rows, pl.ds(TILE, TILE)], slot.at[:, pl.ds(4 * TILE, TILE)], condition)

    corner_slot = corner_in.at[own, pl.ds(pl.multiple_of(chip * TILE, TILE), TILE)]
    for k in range(4):
        stage(front.at[pl.ds(0, TILE), pl.ds(4 * k * TILE, TILE)], corner_slot.at[:, pl.ds(k * TILE, TILE)], core == 0)
    stage_row(0, gathered.at[own, 3 * chip + 1], core == 1)
    stage_row(1, gathered.at[own, 3 * chip + 2 * core])
    for k in range(4):
        stage(front.at[:, pl.ds(4 * k * TILE, TILE)], own_rows.at[:, pl.ds(k * TILE, TILE)])

    barrier = pltpu.get_barrier_semaphore()
    for device in (sibling, right, left, partner):
        pl.semaphore_signal(barrier, inc=1, device_id=device, device_id_type=MESH)
    pl.semaphore_wait(barrier, 4)
    for condition, copy in staged:
        when(condition, copy.wait)

    @pl.when((core == 0) & (chip == 0) & (half == 0))
    def _():
        corner_in[0, 0:1, TILE : 2 * TILE] = weights[0:1, 0:TILE]

    sends = []

    def remote(ref, send_sem, recv_sem, device):
        return pltpu.make_async_remote_copy(
            src_ref=ref, dst_ref=ref, send_sem=send_sem, recv_sem=recv_sem, device_id=device, device_id_type=MESH
        )

    def first_pieces(child, offset):
        k = chip_at(offset)
        rows = pl.ds(pl.multiple_of(k * TILE, TILE), TILE)
        refs = (
            (None, corner_in.at[child, rows, pl.ds(0, 2 * TILE)]),
            (k >= 2, corner_in.at[child, rows, pl.ds(2 * TILE, 2 * TILE)]),
            (k == 0, gathered.at[child, 0]),
        )
        return [(condition, ref, first_recv.at[child, k, n]) for n, (condition, ref) in enumerate(refs)]

    counts = {"first": 0, "bulk": 0}

    def start(kind, pool, build, device):
        number = counts[kind]
        counts[kind] += 1

        def make():
            condition, ref, recv_sem = build()
            return condition, remote(ref, pool.at[number], recv_sem, device)

        sends.append((kind, make))
        condition, copy = make()
        when(condition, copy.start)

    def first_send_to(child, offset, devices, pieces=(0, 1, 2)):
        for device in devices:
            for n in pieces:
                start("first", first_send, lambda n=n: first_pieces(child, offset)[n], device)

    def first_arrive(child, offset):
        for condition, ref, recv_sem in first_pieces(child, offset):
            when(condition, remote(ref, first_send.at[0], recv_sem, partner).wait_recv)

    def bulk_pieces(child, offset, from_core):
        k = chip_at(offset)
        pieces = []
        for i in range(2):
            a = 3 * k + lax.select(from_core == 1, 1 + i, 0)
            condition = (from_core == 1) if i == 1 else ((from_core == 1) | (k != 0))
            for q in range(2):
                pieces.append((condition, gathered.at[child, a, pl.ds(q * 64, 64)], bulk_recv.at[child, a, q]))
        return pieces

    def bulk_send_to(child, offset, devices, only=None):
        for device in devices:
            for n in range(4):
                if only is None or only == n % 2:
                    start("bulk", bulk_send, lambda n=n: bulk_pieces(child, offset, core)[n], device)

    def bulk_arrive(child, offset, from_core):
        for condition, ref, recv_sem in bulk_pieces(child, offset, from_core):
            when(condition, remote(ref, bulk_send.at[0], recv_sem, partner).wait_recv)

    @pl.when(core == 0)
    def _():
        first_send_to(own, 0, (right, left, sibling, partner))
        first_arrive(own, -1)
        first_send_to(own, -1, (right,), (0, 2))
        first_arrive(own, 1)
        first_send_to(own, 1, (left,), (1,))
        first_arrive(other, 0)
        first_send_to(other, 0, (right, left))
        first_send_to(own, -1, (partner,))
        first_send_to(own, 1, (partner,))
        first_send_to(other, 0, (partner,))
        first_arrive(other, -1)
        first_send_to(other, -1, (right,), (0, 2))
        first_arrive(other, 1)
        first_send_to(other, 1, (left,), (1,))
        first_send_to(other, -1, (partner,))
        first_send_to(other, 1, (partner,))

    bulk_send_to(own, 0, (sibling, right, left, partner))

    @pl.when(core == 0)
    def _():
        for child in (own, other):
            first_arrive(child, 2)
            first_send_to(child, 2, (partner,))

    @pl.when(core == 1)
    def _():
        for child in (own, other):
            for offset in (0, -1, 1, 2):
                first_arrive(child, offset)

    def row_copy(r, g):
        return pltpu.make_async_remote_copy(
            src_ref=front.at[pl.ds(r * TILE, TILE), pl.ds((4 * g + 1) * TILE, 3 * TILE)],
            dst_ref=sibling_rows.at[pl.ds(r * TILE, TILE), pl.ds(3 * g * TILE, 3 * TILE)],
            send_sem=row_send.at[r, g],
            recv_sem=row_recv.at[r, g],
            device_id=sibling,
            device_id_type=MESH,
        )

    def after_block(k):
        if k == 0:
            bulk_arrive(other, 0, core)
            bulk_send_to(other, 0, (right, left, partner))
            for g in range(4):
                row_copy(1, g).start()

            @pl.when(core == 1)
            def _():
                for g in range(4):
                    row_copy(0, g).start()

        if k == 1:
            bulk_arrive(own, -1, core)
            bulk_send_to(own, -1, (right,), 0)
            bulk_send_to(own, -1, (partner,))
            bulk_arrive(own, 1, core)
            bulk_send_to(own, 1, (left,), 1)
            bulk_send_to(own, 1, (partner,))
        if k == 3:
            bulk_arrive(other, -1, core)
            bulk_send_to(other, -1, (right,), 0)
            bulk_send_to(other, -1, (partner,))
            bulk_arrive(other, 1, core)
            bulk_send_to(other, 1, (left,), 1)
            bulk_send_to(other, 1, (partner,))

    corner[...] = corner_in[...]
    for k in range(4):
        here = slice(k * TILE, (k + 1) * TILE)
        for child in range(2):
            start_block(corner[child, here, here], mat.at[child], tile.at[child], upper.at[child])

        @pl.loop(0, TILE // 8)
        def _(step):
            for child in range(2):
                factor_panel(step, mat.at[child], tile.at[child], upper.at[child], inv.at[child])

        for child in range(2):
            finish_block(k, corner.at[child], inv.at[child], factors.at[child])
        after_block(k)

    for child in range(2):
        for j in range(3):
            solver[child, j] = right_stack(*halves(factors[child, j]))

    def solve(child, columns):
        one = stack_dot(left_stack(*halves(columns[:, : 2 * TILE])), solver[child, 0])
        one_high, one_low = halves(one)
        two = columns[:, 2 * TILE :] - stack_dot(left_stack(one_high, one_low), solver[child, 2])
        two = stack_dot(left_stack(*halves(two)), solver[child, 1])
        return one, two

    row = lax.broadcasted_iota(jnp.int32, (TILE, TILE), 0)
    col = lax.broadcasted_iota(jnp.int32, (TILE, TILE), 1)
    near = jnp.where(jnp.abs(row - col) == 1, 1.0, 0.0)
    total = jnp.where(row == col, corner_in[0, 0:1, TILE : 2 * TILE] + 4.0, 0.0) - near
    for child in range(2):
        one_high, one_low = halves(jnp.concatenate(solve(child, gathered[child, 0, :, : 4 * TILE]), axis=1))
        lead[child] = right_stack(one_high, one_low)
        total = total + (gathered[child, 0, :, 4 * TILE :] - stack_dot(left_stack(one_high, one_low), lead[child]))
    top[...] = total
    start_block(total, mat.at[0], tile.at[0], upper.at[0])

    @pl.loop(0, TILE // 8)
    def _(step):
        factor_panel(step, mat.at[0], tile.at[0], upper.at[0], top_inv)

    one, two = solve(own, own_rows[...])
    own_panel[:, : 2 * TILE] = one
    own_panel[:, 2 * TILE :] = two

    def panels(child, offset):
        rows = pl.ds(3 * chip_at(offset), 3)
        block = gathered[child, rows].reshape(3 * TILE, 5 * TILE)
        whole_high, whole_low = halves(jnp.concatenate(solve(child, block[:, : 4 * TILE]), axis=1))
        high[child, rows] = whole_high.reshape(3, TILE, 4 * TILE)
        low[child, rows] = whole_low.reshape(3, TILE, 4 * TILE)
        product = stack_dot(left_stack(whole_high, whole_low), lead[child])
        column[child, rows] = (block[:, 4 * TILE :] - product).reshape(3, TILE, TILE)

    for offset in (0, -1, 1):
        for child in (own, other):
            bulk_arrive(child, offset, 1 - core)
            panels(child, offset)
    for child in (own, other):
        bulk_arrive(child, 2, core)
        bulk_send_to(child, 2, (partner,))
    for child in (own, other):
        bulk_arrive(child, 2, 1 - core)
        panels(child, 2)

    def sent(kind):
        for name, make in sends:
            if name == kind:
                condition, copy = make()
                when(condition, copy.wait_send)

    pl.when(core == 0)(lambda: sent("first"))
    sent("bulk")
    for g in range(4):
        row_copy(1, g).wait()

    @pl.when(core == 1)
    def _():
        for g in range(4):
            row_copy(0, g).wait()


def finish_block(k, corner, inv, factors):
    here = slice(k * TILE, (k + 1) * TILE)
    inverse = inv[...]
    level, place = divmod(k, 2)
    if place == 0:
        factors[level, 0:TILE, 0:TILE] = inverse
        factors[level, 0:TILE, TILE:] = jnp.zeros((TILE, TILE), f32)
    else:
        before = slice((k - 1) * TILE, k * TILE)
        middle = exact_dot(corner[here, before], factors[level, 0:TILE, 0:TILE], NN)
        factors[level, TILE:, 0:TILE] = -exact_dot(inverse, middle, NN)
        factors[level, TILE:, TILE:] = inverse
    if k < 3:
        rest = slice((k + 1) * TILE, 4 * TILE)
        below = exact_dot(corner[rest, here], inverse, NT)
        corner[rest, here] = below
        corner[rest, rest] -= exact_dot(below, below, NT)
        if level == 0:
            cut = (1 - place) * TILE
            factors[2, :, place * TILE : (place + 1) * TILE] = below[cut:, :]


def gather_factor(front, weights):
    rows, width = front.shape
    local = pl.BlockSpec(memory_space=pltpu.VMEM)
    anywhere = pl.BlockSpec(memory_space=pl.ANY)
    return pl.pallas_call(
        gather_factor_kernel,
        out_shape=(
            jax.ShapeDtypeStruct((rows, 12 * TILE), f32),
            jax.ShapeDtypeStruct((2, 12, TILE, 4 * TILE), bf16),
            jax.ShapeDtypeStruct((2, 12, TILE, 4 * TILE), bf16),
            jax.ShapeDtypeStruct((2, 12, TILE, TILE), f32),
            jax.ShapeDtypeStruct((TILE, TILE), f32),
            jax.ShapeDtypeStruct((TILE, TILE), f32),
            jax.ShapeDtypeStruct((rows, 4 * TILE), f32),
        ),
        in_specs=[anywhere, local],
        out_specs=(anywhere, local, local, local, local, local, local),
        scratch_shapes=[
            pltpu.VMEM((2, 12, TILE, 5 * TILE), f32),
            pltpu.VMEM((2, 4 * TILE, 4 * TILE), f32),
            pltpu.VMEM((2, 4 * TILE, 4 * TILE), f32),
            pltpu.VMEM((rows, 4 * TILE), f32),
            pltpu.VMEM((2, 3, 2 * TILE, 2 * TILE), f32),
            pltpu.VMEM((2, 3, 2 * TILE, 6 * TILE), bf16),
            pltpu.VMEM((2, TILE, 12 * TILE), bf16),
            pltpu.VMEM((2, TILE, TILE), f32),
            pltpu.VMEM((2, TILE, 2 * TILE), f32),
            pltpu.VMEM((2, 8, 2 * TILE), f32),
            pltpu.VMEM((2, 8, 2 * TILE), f32),
            pltpu.SemaphoreType.DMA((20,)),
            pltpu.SemaphoreType.DMA((60,)),
            pltpu.SemaphoreType.DMA((2, 4, 3)),
            pltpu.SemaphoreType.DMA((80,)),
            pltpu.SemaphoreType.DMA((2, 12, 2)),
            pltpu.SemaphoreType.DMA((2, 4)),
            pltpu.SemaphoreType.DMA((2, 4)),
        ],
        compiler_params=pltpu.CompilerParams(
            collective_id=0, has_side_effects=True, vmem_limit_bytes=34 * 2**20
        ),
        name="gather_factor",
    )(front, weights)


def assemble_kernel(
    index, front, sibling_rows, weights, high, low, column, top, top_inv, own_panel,
    leaf_panel, parent_panel, parent_update,
    own_front, sib_front, parent, parent_high, parent_low, child_of, row_sem,
):
    leaf = lax.axis_index("leaf")
    front_id = lax.axis_index("front")
    half = lax.rem(leaf, 2)
    first = leaf - half
    row_loads = [
        pltpu.make_async_copy(front, own_front, row_sem.at[0]),
        pltpu.make_async_copy(sibling_rows, sib_front, row_sem.at[1]),
    ]
    for copy in row_loads:
        copy.start()
    leaf_panel[...] = own_panel[...]

    @pl.loop(0, 32)
    def _(p):
        child_of[0, p] = -1
        child_of[1, p] = -1

    for child in range(2):
        for a in range(12):
            child_of[child, index[first + child, a]] = a

    row = lax.broadcasted_iota(jnp.int32, (TILE, TILE), 0)
    col = lax.broadcasted_iota(jnp.int32, (TILE, TILE), 1)
    near = jnp.where(jnp.abs(row - col) == 1, 1.0, 0.0)
    above = jnp.where((row == 0) & (col == TILE - 1), 1.0, 0.0)
    under = jnp.where((row == TILE - 1) & (col == 0), 1.0, 0.0)

    @pl.loop(0, 32)
    def _(p):
        total = jnp.zeros((TILE, TILE), f32)
        for child in range(2):
            a = child_of[child, p]
            total = total + jnp.where(a >= 0, column[child, jnp.maximum(a, 0)], 0.0)
        parent[p] = total

    parent[0] = top[...]
    parent[1] -= above

    last = right_stack(*halves(top_inv[...]))
    for q in range(8):
        block = parent[4 * q : 4 * q + 4].reshape(4 * TILE, TILE)
        done = stack_dot(left_stack(*halves(block)), last)
        parent[4 * q : 4 * q + 4] = done.reshape(4, TILE, TILE)
        done_high, done_low = halves(done)
        parent_high[4 * q * TILE : 4 * (q + 1) * TILE, :] = done_high
        parent_low[4 * q * TILE : 4 * (q + 1) * TILE, :] = done_low

    place = 4 * front_id + 2 * half
    parent_panel[...] = parent[pl.ds(place, 2)].reshape(2 * TILE, TILE)
    here = pl.ds(pl.multiple_of(place * TILE, TILE), 2 * TILE)
    mine = left_stack(parent_high[here, :], parent_low[here, :])
    for start in range(TILE, 32 * TILE, 4 * TILE):
        stop = min(start + 4 * TILE, 32 * TILE)
        there = right_stack(parent_high[start:stop, :], parent_low[start:stop, :])
        parent_update[:, start - TILE : stop - TILE] = -stack_dot(mine, there)

    def columns_of(p):
        return pl.ds(pl.multiple_of((p - 1) * TILE, TILE), TILE)

    for copy in row_loads:
        copy.wait()
    for kin in range(2):
        child = half if kin == 0 else 1 - half
        source = own_front if kin == 0 else sib_front
        for r in range(2):
            a = child_of[child, place + r]
            rows = pl.ds(r * TILE, TILE)

            @pl.when(a >= 0)
            def _():
                local = 4 * lax.div(a, 3) + lax.rem(a, 3) + 1 - 2 * front_id
                source_rows = pl.ds(pl.multiple_of(local * TILE, TILE), TILE)
                lead = left_stack(high[child, a], low[child, a])
                for g in range(4):
                    others = right_stack(
                        high[child, pl.ds(3 * g, 3)].reshape(3 * TILE, 4 * TILE),
                        low[child, pl.ds(3 * g, 3)].reshape(3 * TILE, 4 * TILE),
                    )
                    product = stack_dot(lead, others)
                    for m in range(3):
                        b = 3 * g + m
                        p = index[first + child, b]
                        t = 4 * g + m + 1 if kin == 0 else b
                        value = source[source_rows, t * TILE : (t + 1) * TILE] - product[:, m * TILE : (m + 1) * TILE]
                        if b == 0:
                            continue
                        parent_update[rows, columns_of(p)] += value

    for r in range(2):
        p = place + r
        rows = slice(r * TILE, (r + 1) * TILE)
        own_weights = weights[0:1, r * TILE : (r + 1) * TILE]
        inside = p < SEP2_TILES

        @pl.when(p >= 1)
        def _():
            extra = jnp.where(inside, 1.0, 0.0)
            parent_update[rows, columns_of(p)] += jnp.where(row == col, own_weights + 4.0 * extra, 0.0) - near * extra

        @pl.when((p >= 2) & inside)
        def _():
            parent_update[rows, columns_of(p - 1)] -= above

        @pl.when(p + 1 < SEP2_TILES)
        def _():
            parent_update[rows, columns_of(p + 1)] -= under


def assemble(index, front, weights, sibling_rows, *rest):
    rows, width = front.shape
    anywhere = pl.BlockSpec(memory_space=pl.ANY)
    local = pl.BlockSpec(memory_space=pltpu.VMEM)
    return pl.pallas_call(
        assemble_kernel,
        out_shape=(
            jax.ShapeDtypeStruct((rows, 4 * TILE), f32),
            jax.ShapeDtypeStruct((rows, TILE), f32),
            jax.ShapeDtypeStruct((rows, 31 * TILE), f32),
        ),
        in_specs=[pl.BlockSpec(memory_space=pltpu.SMEM), anywhere, anywhere] + [local] * 7,
        out_specs=(local, local, local),
        scratch_shapes=[
            pltpu.VMEM((rows, width), f32),
            pltpu.VMEM((rows, 12 * TILE), f32),
            pltpu.VMEM((32, TILE, TILE), f32),
            pltpu.VMEM((32 * TILE, TILE), bf16),
            pltpu.VMEM((32 * TILE, TILE), bf16),
            pltpu.SMEM((2, 32), jnp.int32),
            pltpu.SemaphoreType.DMA((2,)),
        ],
        compiler_params=pltpu.CompilerParams(vmem_limit_bytes=30 * 2**20),
        name="assemble",
    )(index, front, sibling_rows, weights, *rest)


def on_device(leaf_fronts, screen_weights, parent_tile_index):
    front = leaf_fronts[0, 0]
    weights = screen_weights[0]
    index = parent_tile_index[:, 0]
    leaf_panel, parent_panel, parent_update = assemble(index, front, weights, *gather_factor(front, weights))
    return leaf_panel[None, None], parent_panel[None, None], parent_update[None, None]


def solution(mesh):
    rows = P("leaf", None, "front", None)
    return jax.shard_map(
        on_device,
        mesh=mesh,
        in_specs=(rows, P("leaf", None, "front"), P()),
        out_specs=(rows, rows, rows),
        check_vma=False,
    )
```

time: 134 us -> 95.2 us (0.71)
  the two profiles are of different devices: /device:TPU:160 before, /device:TPU:253 now
where the time goes in v1:
time: 95.2 us; the launch traced here: 95 us
  Pallas kernels  91.2 us (96%)
  local copies, waits for them, and re-layouts  3.04 us (3%)
    pallas_call x1, Pallas kernels, gather_factor(): pl.pallas_call(gather_factor_kernel, out_shape=(jax.ShapeDtypeStruct((row...  78.4 us
    pallas_call x1, Pallas kernels, assemble(): pl.pallas_call(assemble_kernel, out_shape=(jax.ShapeDtypeStruct((rows, 4...  12.7 us
    unnamed x7, local copies, waits for them, and re-layouts  3.04 us

profile of v1, /device:TPU:253, one launch (start us, length us, event | category | flops | bytes accessed | tf_op | source)
XLA Modules:
  0.0 95.0 jit_solution(609448059801788583)
XLA Ops:
  0.6 0.8 copy.6
  1.4 0.0 copy-start
  1.4 1.6 %copy-done = f32[1,1,256,2048]{3,2,1,0:T(8,128)S(1)} copy-done((f32[1,1,256,2048]{3,2,1,0:T(8,128)S(1)}, f32[1,1,256,2048]{3,2,1,0:T(8,128)}, u32[]{:S(2)}) %copy-start) | copy-done | bytes 2097176
  3.0 0.0 copy-start.2
  3.0 0.7 copy-done.2
  3.7 0.0 copy-start.1
  3.7 78.4 %gather_factor.1 = (f32[256,1536]{1,0:T(8,128)S(1)}, bf16[2,12,128,512]{3,2,1,0:T(8,128)(2,1)S(1)}, bf16[2,12,128,512]{3,2,1,0:T(8,128)(2,1)S(1)}, f32[2,12,128,...) custom-call(f32[256,2048]{1,0:T(8,128)S(1)} %bitcast.6, ...), custom_call_target="tpu_custom_call" | custom-call | tf_op jit(solution)/shard_map/gather_factor/pallas_call | solution.py:402
  82.1 0.0 copy-done.1
  82.1 12.7 %assemble.1 = (f32[256,512]{1,0:T(8,128)}, f32[256,128]{1,0:T(8,128)}, f32[256,3968]{1,0:T(8,128)}) custom-call(s32[32,12]{1,0:T(8,128)S(1)} %bitcast.8, f32[256,2048]{1,0:T(8,128)S(1)} %bitcast.7, f32[256,1536]{1,0:T(8,128)S(1)} %get-tuple-element.13.sibling_rows, f32[1,256]{1,0:T(1,128)S(1)} %bitcast.10, ...), custom_call_target="tpu_custom_call" | custom-call | tf_op jit(solution)/shard_map/assemble/pallas_call | solution.py:559
Async XLA Ops:
  1.4 1.6 %copy-start = (f32[1,1,256,2048]{3,2,1,0:T(8,128)S(1)}, f32[1,1,256,2048]{3,2,1,0:T(8,128)}, u32[]{:S(2)}) copy-start(f32[1,1,256,2048]{3,2,1,0:T(8,128)} %param.3) | copy-start | bytes 6291460
  3.0 0.7 copy-start.2
  3.7 78.5 %copy-start.1 = (f32[1,1,256,2048]{3,2,1,0:T(8,128)S(1)}, f32[1,1,256,2048]{3,2,1,0:T(8,128)}, u32[]{:S(2)}) copy-start(f32[1,1,256,2048]{3,2,1,0:T(8,128)} %param.3) | copy-start | bytes 6291460

commit v2 on v1

--- a/solution.py
+++ b/solution.py
@@ -69,22 +69,18 @@
     right = jnp.concatenate([high, mid, high, low, high, mid], axis=0)
     mat[...] -= lax.dot_general(left, right, TN, preferred_element_type=f32)
     rows = tile[...]
+    cols = [
+        jnp.take_along_axis(rows[:, :TILE], jnp.full((8, TILE), base + j, jnp.int32), axis=1) for j in range(8)
+    ]
+    done = []
+    packed = jnp.zeros((8, 2 * TILE), f32)
     entry = {}
     for j in range(8):
-        picked = jnp.take_along_axis(rows[:, :TILE], jnp.full((8, TILE), base + j, jnp.int32), axis=1)
-        for i in range(j, 8):
-            entry[i, j] = jnp.broadcast_to(picked[i : i + 1, :], (8, TILE))
-    done = []
-    packed = jnp.zeros((8, 2 * TILE), f32)
-    for j in range(8):
-        pivot = entry[j, j]
-        scale = lax.rsqrt(pivot)
-        scale = scale * (1.5 - 0.5 * pivot * scale * scale)
-        for i in range(j + 1, 8):
-            entry[i, j] = entry[i, j] * scale
-        for i in range(j + 1, 8):
-            for k in range(j + 1, i + 1):
-                entry[i, k] = entry[i, k] - entry[i, j] * entry[k, j]
+        scale = lax.rsqrt(jnp.broadcast_to(cols[j][j : j + 1, :], (8, TILE)))
+        column = cols[j] * scale
+        for k in range(j + 1, 8):
+            entry[k, j] = jnp.broadcast_to(column[k : k + 1, :], (8, TILE))
+            cols[k] = cols[k] - column * entry[k, j]
         row = jnp.broadcast_to(rows[j : j + 1, :], (8, 2 * TILE))
         for p in range(j):
             row = row - twice(entry[j, p]) * done[p]
@@ -101,10 +97,15 @@
     tile[...] = total
 
 
+PASS_ON = (
+((1, (1, 0, 0)), (2, (0, -1, 0)), (2, (0, 1, 0)), (4, (1, -1, 0)), (4, (1, 1, 0)), (5, (0, 2, 0)), (7, (1, 2, 0))),
+((1, (1, 0, 0)), (1, (1, 0, 1)), (3, (0, -1, 0)), (3, (0, 1, 0)), (4, (0, -1, 1)), (4, (0, 1, 1)), (8, (1, -1, 0)), (8, (1, 1, 0)), (8, (1, -1, 1)), (8, (1, 1, 1)), (9, (0, 2, 0)), (9, (0, 2, 1)), (10, (1, 2, 0)), (10, (1, 2, 1))))
+
+
 def gather_factor_kernel(
-    front, weights,
+    front, weight_row,
     sibling_rows, high, low, column, top, top_inv, own_panel,
-    gathered, corner_in, corner, own_rows, factors, solver, lead, inv, mat, tile, upper,
+    gathered, corner_in, corner, own_rows, factors, solver, lead, inv, mat, tile, upper, weights,
     local_sem, first_send, first_recv, bulk_send, bulk_recv, row_send, row_recv,
 ):
     leaf = lax.axis_index("leaf")
@@ -122,6 +123,10 @@
     right = (leaf, chip_at(1) * 2 + core)
     left = (leaf, chip_at(-1) * 2 + core)
     partner = (leaf, front_id + 1 - 2 * core)
+    opposite = (leaf, chip_at(2) * 2 + core)
+    sibling_right = (sibling[0], right[1])
+    sibling_left = (sibling[0], left[1])
+    sibling_opposite = (sibling[0], opposite[1])
 
     staged = []
 
@@ -150,10 +155,13 @@
     for k in range(4):
         stage(front.at[:, pl.ds(4 * k * TILE, TILE)], own_rows.at[:, pl.ds(k * TILE, TILE)])
 
+    stage(weight_row, weights)
+
     barrier = pltpu.get_barrier_semaphore()
-    for device in (sibling, right, left, partner):
+    greeted = (sibling, right, left, opposite, sibling_right, sibling_left, sibling_opposite, partner)
+    for device in greeted:
         pl.semaphore_signal(barrier, inc=1, device_id=device, device_id_type=MESH)
-    pl.semaphore_wait(barrier, 4)
+    pl.semaphore_wait(barrier, len(greeted))
     for condition, copy in staged:
         when(condition, copy.wait)
 
@@ -168,17 +176,19 @@
             src_ref=ref, dst_ref=ref, send_sem=send_sem, recv_sem=recv_sem, device_id=device, device_id_type=MESH
         )
 
+    def top_pieces(child):
+        refs = (corner_in.at[child, pl.ds(0, TILE), pl.ds(0, TILE)], corner_in.at[child, pl.ds(0, 8), pl.ds(TILE, TILE)])
+        return [(None, ref, first_recv.at[child, 0, n]) for n, ref in enumerate(refs)]
+
     def first_pieces(child, offset):
         k = chip_at(offset)
         rows = pl.ds(pl.multiple_of(k * TILE, TILE), TILE)
-        refs = (
-            (None, corner_in.at[child, rows, pl.ds(0, 2 * TILE)]),
-            (k >= 2, corner_in.at[child, rows, pl.ds(2 * TILE, 2 * TILE)]),
-            (k == 0, gathered.at[child, 0]),
+        return (
+            (k >= 1, corner_in.at[child, rows, pl.ds(0, 2 * TILE)], first_recv.at[child, k, 0]),
+            (k >= 2, corner_in.at[child, rows, pl.ds(2 * TILE, 2 * TILE)], first_recv.at[child, k, 1]),
         )
-        return [(condition, ref, first_recv.at[child, k, n]) for n, (condition, ref) in enumerate(refs)]
-
-    counts = {"first": 0, "bulk": 0}
+
+    counts = {"top": 0, "pass": 16, "first": 18, 0: 0, 1: 0}
 
     def start(kind, pool, build, device):
         number = counts[kind]
@@ -192,7 +202,16 @@
         condition, copy = make()
         when(condition, copy.start)
 
-    def first_send_to(child, offset, devices, pieces=(0, 1, 2)):
+    def top_send_to(kind, child, devices):
+        for device in devices:
+            for n in range(2):
+                start(kind, first_send, lambda n=n: top_pieces(child)[n], device)
+
+    def top_arrive(child):
+        for condition, ref, recv_sem in top_pieces(child):
+            remote(ref, first_send.at[0], recv_sem, partner).wait_recv()
+
+    def first_send_to(child, offset, devices, pieces=(0, 1)):
         for device in devices:
             for n in pieces:
                 start("first", first_send, lambda n=n: first_pieces(child, offset)[n], device)
@@ -201,58 +220,75 @@
         for condition, ref, recv_sem in first_pieces(child, offset):
             when(condition, remote(ref, first_send.at[0], recv_sem, partner).wait_recv)
 
-    def bulk_pieces(child, offset, from_core):
-        k = chip_at(offset)
-        pieces = []
-        for i in range(2):
-            a = 3 * k + lax.select(from_core == 1, 1 + i, 0)
-            condition = (from_core == 1) if i == 1 else ((from_core == 1) | (k != 0))
+    def bulk_piece(child, offset, from_core, i, q):
+        a = 3 * chip_at(offset) + from_core * (1 + i)
+        return None, gathered.at[child, a, pl.ds(q * 64, 64)], bulk_recv.at[child, a, q]
+
+    def bulk_send_to(kind, child, offset, i, q, devices):
+        for device in devices:
+            start(kind, bulk_send, lambda: bulk_piece(child, offset, kind, i, q), device)
+
+    def bulk_arrive(child, offset, from_core, i, q):
+        condition, ref, recv_sem = bulk_piece(child, offset, from_core, i, q)
+        when(condition, remote(ref, bulk_send.at[0], recv_sem, partner).wait_recv)
+
+    def bulk_step(kind, child, offset, i):
+        for q in range(2):
+            bulk_arrive(child, offset, kind, i, q)
+            if offset == 0:
+                onward = (right, left)
+            elif offset == -1 and q == 0:
+                onward = (right,)
+            elif offset == 1 and q == 1:
+                onward = (left,)
+            else:
+                onward = ()
+            bulk_send_to(kind, child, offset, i, q, onward + (partner,))
+
+    def own_bulk(kind):
+        for i in range(1 + kind):
             for q in range(2):
-                pieces.append((condition, gathered.at[child, a, pl.ds(q * 64, 64)], bulk_recv.at[child, a, q]))
-        return pieces
-
-    def bulk_send_to(child, offset, devices, only=None):
-        for device in devices:
-            for n in range(4):
-                if only is None or only == n % 2:
-                    start("bulk", bulk_send, lambda n=n: bulk_pieces(child, offset, core)[n], device)
-
-    def bulk_arrive(child, offset, from_core):
-        for condition, ref, recv_sem in bulk_pieces(child, offset, from_core):
-            when(condition, remote(ref, bulk_send.at[0], recv_sem, partner).wait_recv)
+                bulk_send_to(kind, own, 0, i, q, (sibling, right, left, partner))
+
+    @pl.when((core == 0) & (chip == 0))
+    def _():
+        top_send_to("top", own, (sibling, right, left, opposite, sibling_right, sibling_left, sibling_opposite, partner))
 
     @pl.when(core == 0)
     def _():
-        first_send_to(own, 0, (right, left, sibling, partner))
-        first_arrive(own, -1)
-        first_send_to(own, -1, (right,), (0, 2))
-        first_arrive(own, 1)
-        first_send_to(own, 1, (left,), (1,))
+        first_send_to(own, 0, (sibling, right, left, opposite, partner))
+        own_bulk(0)
         first_arrive(other, 0)
-        first_send_to(other, 0, (right, left))
-        first_send_to(own, -1, (partner,))
-        first_send_to(own, 1, (partner,))
-        first_send_to(other, 0, (partner,))
-        first_arrive(other, -1)
-        first_send_to(other, -1, (right,), (0, 2))
-        first_arrive(other, 1)
-        first_send_to(other, 1, (left,), (1,))
-        first_send_to(other, -1, (partner,))
-        first_send_to(other, 1, (partner,))
-
-    bulk_send_to(own, 0, (sibling, right, left, partner))
-
-    @pl.when(core == 0)
-    def _():
+        first_send_to(other, 0, (right, left, opposite))
+
+        @pl.when(chip != 0)
+        def _():
+            top_arrive(own)
+            top_send_to("pass", own, (partner,))
+
+        top_arrive(other)
+        top_send_to("first", other, (partner,))
+
+    @pl.when(core == 1)
+    def _():
+        own_bulk(1)
         for child in (own, other):
-            first_arrive(child, 2)
-            first_send_to(child, 2, (partner,))
-
-    @pl.when(core == 1)
-    def _():
-        for child in (own, other):
-            for offset in (0, -1, 1, 2):
+            top_arrive(child)
+
+    def pass_first():
+        @pl.when(core == 0)
+        def _():
+            first_send_to(other, 0, (partner,))
+            for child, offset in ((own, -1), (own, 1), (own, 2), (other, -1), (other, 1), (other, 2)):
                 first_arrive(child, offset)
+                first_send_to(child, offset, (partner,))
+
+    def last_first():
+        @pl.when(core == 1)
+        def _():
+            for child in (own, other):
+                for offset in (0, -1, 1, 2):
+                    first_arrive(child, offset)
 
     def row_copy(r, g):
         return pltpu.make_async_remote_copy(
@@ -264,47 +300,46 @@
             device_id_type=MESH,
         )
 
-    def after_block(k):
-        if k == 0:
-            bulk_arrive(other, 0, core)
-            bulk_send_to(other, 0, (right, left, partner))
+    def start_rows():
+        for g in range(4):
+            row_copy(1, g).start()
+
+        @pl.when(core == 1)
+        def _():
             for g in range(4):
-                row_copy(1, g).start()
-
-            @pl.when(core == 1)
-            def _():
-                for g in range(4):
-                    row_copy(0, g).start()
-
-        if k == 1:
-            bulk_arrive(own, -1, core)
-            bulk_send_to(own, -1, (right,), 0)
-            bulk_send_to(own, -1, (partner,))
-            bulk_arrive(own, 1, core)
-            bulk_send_to(own, 1, (left,), 1)
-            bulk_send_to(own, 1, (partner,))
-        if k == 3:
-            bulk_arrive(other, -1, core)
-            bulk_send_to(other, -1, (right,), 0)
-            bulk_send_to(other, -1, (partner,))
-            bulk_arrive(other, 1, core)
-            bulk_send_to(other, 1, (left,), 1)
-            bulk_send_to(other, 1, (partner,))
-
-    corner[...] = corner_in[...]
+                row_copy(0, g).start()
+
+    def pass_on(point):
+        for kind in range(2):
+            listed = [step for when_, step in PASS_ON[kind] if when_ == point]
+            if listed:
+
+                @pl.when(core == kind)
+                def _():
+                    for sib, offset, i in listed:
+                        bulk_step(kind, other if sib else own, offset, i)
+
     for k in range(4):
         here = slice(k * TILE, (k + 1) * TILE)
         for child in range(2):
-            start_block(corner[child, here, here], mat.at[child], tile.at[child], upper.at[child])
-
-        @pl.loop(0, TILE // 8)
-        def _(step):
-            for child in range(2):
-                factor_panel(step, mat.at[child], tile.at[child], upper.at[child], inv.at[child])
+            start_block((corner_in if k == 0 else corner)[child, here, here], mat.at[child], tile.at[child], upper.at[child])
+
+        for part in range(2):
+
+            @pl.loop(part * (TILE // 16), (part + 1) * (TILE // 16))
+            def _(step):
+                for child in range(2):
+                    factor_panel(step, mat.at[child], tile.at[child], upper.at[child], inv.at[child])
+
+            if k == 0:
+                (pass_first, last_first)[part]()
+            pass_on(2 * k + part)
+            if (k, part) == (0, 1):
+                start_rows()
+                corner[...] = corner_in[...]
 
         for child in range(2):
             finish_block(k, corner.at[child], inv.at[child], factors.at[child])
-        after_block(k)
 
     for child in range(2):
         for j in range(3):
@@ -315,46 +350,75 @@
         one_high, one_low = halves(one)
         two = columns[:, 2 * TILE :] - stack_dot(left_stack(one_high, one_low), solver[child, 2])
         two = stack_dot(left_stack(*halves(two)), solver[child, 1])
-        return one, two
+        two_high, two_low = halves(two)
+        high_low = (jnp.concatenate([one_high, two_high], axis=1), jnp.concatenate([one_low, two_low], axis=1))
+        return one, two, high_low
+
+    one, two, _ = solve(own, own_rows[...])
+    own_panel[:, : 2 * TILE] = one
+    own_panel[:, 2 * TILE :] = two
+    pass_on(8)
+
+    @pl.when(core == 1)
+    def _():
+        for child in (own, other):
+            for offset in (0, -1, 1, 2):
+                for q in range(2):
+                    bulk_arrive(child, offset, 0, 0, q)
 
     row = lax.broadcasted_iota(jnp.int32, (TILE, TILE), 0)
     col = lax.broadcasted_iota(jnp.int32, (TILE, TILE), 1)
     near = jnp.where(jnp.abs(row - col) == 1, 1.0, 0.0)
     total = jnp.where(row == col, corner_in[0, 0:1, TILE : 2 * TILE] + 4.0, 0.0) - near
     for child in range(2):
-        one_high, one_low = halves(jnp.concatenate(solve(child, gathered[child, 0, :, : 4 * TILE]), axis=1))
-        lead[child] = right_stack(one_high, one_low)
-        total = total + (gathered[child, 0, :, 4 * TILE :] - stack_dot(left_stack(one_high, one_low), lead[child]))
+        high_low = solve(child, gathered[child, 0, :, : 4 * TILE])[2]
+        lead[child] = right_stack(*high_low)
+        total = total + (gathered[child, 0, :, 4 * TILE :] - stack_dot(left_stack(*high_low), lead[child]))
     top[...] = total
     start_block(total, mat.at[0], tile.at[0], upper.at[0])
 
-    @pl.loop(0, TILE // 8)
-    def _(step):
-        factor_panel(step, mat.at[0], tile.at[0], upper.at[0], top_inv)
-
-    one, two = solve(own, own_rows[...])
-    own_panel[:, : 2 * TILE] = one
-    own_panel[:, 2 * TILE :] = two
-
-    def panels(child, offset):
-        rows = pl.ds(3 * chip_at(offset), 3)
+    def panels(child, k):
+        rows = pl.ds(3 * k, 3)
         block = gathered[child, rows].reshape(3 * TILE, 5 * TILE)
-        whole_high, whole_low = halves(jnp.concatenate(solve(child, block[:, : 4 * TILE]), axis=1))
+        whole_high, whole_low = solve(child, block[:, : 4 * TILE])[2]
         high[child, rows] = whole_high.reshape(3, TILE, 4 * TILE)
         low[child, rows] = whole_low.reshape(3, TILE, 4 * TILE)
         product = stack_dot(left_stack(whole_high, whole_low), lead[child])
         column[child, rows] = (block[:, 4 * TILE :] - product).reshape(3, TILE, TILE)
 
-    for offset in (0, -1, 1):
-        for child in (own, other):
-            bulk_arrive(child, offset, 1 - core)
-            panels(child, offset)
+    def partner_rows(*groups):
+        @pl.when(core == 0)
+        def _():
+            for child, offset in groups:
+                for i in range(2):
+                    for q in range(2):
+                        bulk_arrive(child, offset, 1, i, q)
+
+    partner_rows((own, 0), (other, 0))
+
+    @pl.loop(0, 2)
+    def _(group):
+        for part in range(4):
+            factor_panel(4 * group + part, mat.at[0], tile.at[0], upper.at[0], top_inv)
+        panels(lax.select(group == 0, own, other), chip)
+
+    pass_on(9)
+    partner_rows((own, -1), (own, 1))
+
+    @pl.loop(2, 4)
+    def _(group):
+        for part in range(4):
+            factor_panel(4 * group + part, mat.at[0], tile.at[0], upper.at[0], top_inv)
+        panels(own, chip_at(2 * group - 5))
+
+    pass_on(10)
+    partner_rows((other, -1), (other, 1))
+    for offset in (-1, 1):
+        panels(other, chip_at(offset))
+    pass_on(11)
+    partner_rows((own, 2), (other, 2))
     for child in (own, other):
-        bulk_arrive(child, 2, core)
-        bulk_send_to(child, 2, (partner,))
-    for child in (own, other):
-        bulk_arrive(child, 2, 1 - core)
-        panels(child, 2)
+        panels(child, chip_at(2))
 
     def sent(kind):
         for name, make in sends:
@@ -362,8 +426,23 @@
                 condition, copy = make()
                 when(condition, copy.wait_send)
 
-    pl.when(core == 0)(lambda: sent("first"))
-    sent("bulk")
+    @pl.when(core == 0)
+    def _():
+        sent("first")
+        sent(0)
+
+        @pl.when(chip == 0)
+        def _():
+            sent("top")
+
+        @pl.when(chip != 0)
+        def _():
+            sent("pass")
+
+    @pl.when(core == 1)
+    def _():
+        sent(1)
+
     for g in range(4):
         row_copy(1, g).wait()
 
@@ -410,7 +489,7 @@
             jax.ShapeDtypeStruct((TILE, TILE), f32),
             jax.ShapeDtypeStruct((rows, 4 * TILE), f32),
         ),
-        in_specs=[anywhere, local],
+        in_specs=[pl.BlockSpec(memory_space=pltpu.HBM), pl.BlockSpec(memory_space=pltpu.HBM)],
         out_specs=(anywhere, local, local, local, local, local, local),
         scratch_shapes=[
             pltpu.VMEM((2, 12, TILE, 5 * TILE), f32),
@@ -424,9 +503,10 @@
             pltpu.VMEM((2, TILE, 2 * TILE), f32),
             pltpu.VMEM((2, 8, 2 * TILE), f32),
             pltpu.VMEM((2, 8, 2 * TILE), f32),
+            pltpu.VMEM((1, 2 * TILE), f32),
             pltpu.SemaphoreType.DMA((20,)),
             pltpu.SemaphoreType.DMA((60,)),
-            pltpu.SemaphoreType.DMA((2, 4, 3)),
+            pltpu.SemaphoreType.DMA((2, 4, 2)),
             pltpu.SemaphoreType.DMA((80,)),
             pltpu.SemaphoreType.DMA((2, 12, 2)),
             pltpu.SemaphoreType.DMA((2, 4)),
@@ -440,9 +520,9 @@
 
 
 def assemble_kernel(
-    index, front, sibling_rows, weights, high, low, column, top, top_inv, own_panel,
+    index, front, sibling_rows, weight_row, high, low, column, top, top_inv, own_panel,
     leaf_panel, parent_panel, parent_update,
-    own_front, sib_front, parent, parent_high, parent_low, child_of, row_sem,
+    own_front, sib_front, parent, parent_high, parent_low, weights, child_of, row_sem,
 ):
     leaf = lax.axis_index("leaf")
     front_id = lax.axis_index("front")
@@ -451,6 +531,7 @@
     row_loads = [
         pltpu.make_async_copy(front, own_front, row_sem.at[0]),
         pltpu.make_async_copy(sibling_rows, sib_front, row_sem.at[1]),
+        pltpu.make_async_copy(weight_row, weights, row_sem.at[2]),
     ]
     for copy in row_loads:
         copy.start()
@@ -463,7 +544,7 @@
 
     for child in range(2):
         for a in range(12):
-            child_of[child, index[first + child, a]] = a
+            child_of[child, index[a, 0, first + child]] = a
 
     row = lax.broadcasted_iota(jnp.int32, (TILE, TILE), 0)
     col = lax.broadcasted_iota(jnp.int32, (TILE, TILE), 1)
@@ -525,7 +606,7 @@
                     product = stack_dot(lead, others)
                     for m in range(3):
                         b = 3 * g + m
-                        p = index[first + child, b]
+                        p = index[b, 0, first + child]
                         t = 4 * g + m + 1 if kin == 0 else b
                         value = source[source_rows, t * TILE : (t + 1) * TILE] - product[:, m * TILE : (m + 1) * TILE]
                         if b == 0:
@@ -563,7 +644,9 @@
             jax.ShapeDtypeStruct((rows, TILE), f32),
             jax.ShapeDtypeStruct((rows, 31 * TILE), f32),
         ),
-        in_specs=[pl.BlockSpec(memory_space=pltpu.SMEM), anywhere, anywhere] + [local] * 7,
+        in_specs=[pl.BlockSpec(memory_space=pltpu.SMEM), pl.BlockSpec(memory_space=pltpu.HBM), anywhere]
+        + [pl.BlockSpec(memory_space=pltpu.HBM)]
+        + [local] * 6,
         out_specs=(local, local, local),
         scratch_shapes=[
             pltpu.VMEM((rows, width), f32),
@@ -571,8 +654,9 @@
             pltpu.VMEM((32, TILE, TILE), f32),
             pltpu.VMEM((32 * TILE, TILE), bf16),
             pltpu.VMEM((32 * TILE, TILE), bf16),
+            pltpu.VMEM((1, 2 * TILE), f32),
             pltpu.SMEM((2, 32), jnp.int32),
-            pltpu.SemaphoreType.DMA((2,)),
+            pltpu.SemaphoreType.DMA((3,)),
         ],
         compiler_params=pltpu.CompilerParams(vmem_limit_bytes=30 * 2**20),
         name="assemble",
@@ -582,7 +666,9 @@
 def on_device(leaf_fronts, screen_weights, parent_tile_index):
     front = leaf_fronts[0, 0]
     weights = screen_weights[0]
-    index = parent_tile_index[:, 0]
+    index = parent_tile_index.transpose(2, 1, 0)
+    front = pltpu.with_memory_space_constraint(front, pltpu.HBM)
+    weights = pltpu.with_memory_space_constraint(weights, pltpu.HBM)
     leaf_panel, parent_panel, parent_update = assemble(index, front, weights, *gather_factor(front, weights))
     return leaf_panel[None, None], parent_panel[None, None], parent_update[None, None]
 

time: 95.2 us -> 81.3 us (0.85)
  the two profiles are of different devices: /device:TPU:253 before, /device:TPU:65 now
where the time goes in v2:
time: 81.3 us; the launch traced here: 81.2 us
  Pallas kernels  79.7 us (98%)
    pallas_call x1, Pallas kernels, gather_factor(): pl.pallas_call(gather_factor_kernel, out_shape=(jax.ShapeDtypeStruct((row...  67.3 us
    pallas_call x1, Pallas kernels, assemble(): pl.pallas_call(assemble_kernel, out_shape=(jax.ShapeDtypeStruct((rows, 4...  12.4 us

profile of v2, /device:TPU:65, one launch (start us, length us, event | category | flops | bytes accessed | tf_op | source)
XLA Modules:
  0.0 81.2 jit_solution(12392357144378866612)
XLA Ops:
  0.6 67.3 %gather_factor.1 = (f32[256,1536]{1,0:T(8,128)S(1)}, bf16[2,12,128,512]{3,2,1,0:T(8,128)(2,1)S(1)}, bf16[2,12,128,512]{3,2,1,0:T(8,128)(2,1)S(1)}, f32[2,12,128,...) custom-call(f32[256,2048]{1,0:T(8,128)} %bitcast.7, ...), custom_call_target="tpu_custom_call" | custom-call | tf_op jit(solution)/shard_map/gather_factor/pallas_call | solution.py:481
  67.9 0.0 copy-start
  67.9 0.7 copy-done
  68.6 12.4 %assemble.1 = (f32[256,512]{1,0:T(8,128)}, f32[256,128]{1,0:T(8,128)}, f32[256,3968]{1,0:T(8,128)}) custom-call(s32[12,1,32]{2,1,0:T(1,128)S(1)} %bitcast.6, f32[256,2048]{1,0:T(8,128)} %bitcast.8, f32[256,1536]{1,0:T(8,128)S(1)} %get-tuple-element.13.sibling_rows, f32[1,256]{1,0:T(1,128)} %bitcast.10, bf16[2,12,128,512]{3,2,1,0:T(8,128)(2,1)S(1)} %get-tuple-element.14.high, ...), custom_call_target="tpu_custom_call" | custom-call | tf_op jit(solution)/shard_map/assemble/pallas_call | solution.py:640
Async XLA Ops:
  67.9 0.7 copy-start

commit v3 on v2

--- a/solution.py
+++ b/solution.py
@@ -98,8 +98,24 @@
 
 
 PASS_ON = (
-((1, (1, 0, 0)), (2, (0, -1, 0)), (2, (0, 1, 0)), (4, (1, -1, 0)), (4, (1, 1, 0)), (5, (0, 2, 0)), (7, (1, 2, 0))),
-((1, (1, 0, 0)), (1, (1, 0, 1)), (3, (0, -1, 0)), (3, (0, 1, 0)), (4, (0, -1, 1)), (4, (0, 1, 1)), (8, (1, -1, 0)), (8, (1, 1, 0)), (8, (1, -1, 1)), (8, (1, 1, 1)), (9, (0, 2, 0)), (9, (0, 2, 1)), (10, (1, 2, 0)), (10, (1, 2, 1))))
+    (
+        (3, (1, 0, 0)),
+        (4, (0, -1, 0)), (4, (0, 1, 0)),
+        (8, (1, -1, 0)), (8, (1, 1, 0)),
+        (9, (0, 2, 0)),
+        (12, (1, 2, 0)),
+    ),
+    (
+        (4, (1, 0, 0)), (4, (1, 0, 1)),
+        (7, (0, -1, 0)), (7, (0, 1, 0)),
+        (8, (0, -1, 1)), (8, (0, 1, 1)),
+        (14, (1, -1, 0)), (14, (1, 1, 0)),
+        (15, (1, -1, 1)), (15, (1, 1, 1)),
+        (19, (0, 2, 0)), (19, (0, 2, 1)),
+        (21, (1, 2, 0)), (21, (1, 2, 1)),
+    ),
+)
+ROW_POINT = 1
 
 
 def gather_factor_kernel(
@@ -324,19 +340,21 @@
         for child in range(2):
             start_block((corner_in if k == 0 else corner)[child, here, here], mat.at[child], tile.at[child], upper.at[child])
 
-        for part in range(2):
-
-            @pl.loop(part * (TILE // 16), (part + 1) * (TILE // 16))
+        for part in range(4):
+
+            @pl.loop(part * (TILE // 32), (part + 1) * (TILE // 32))
             def _(step):
                 for child in range(2):
                     factor_panel(step, mat.at[child], tile.at[child], upper.at[child], inv.at[child])
 
-            if k == 0:
-                (pass_first, last_first)[part]()
-            pass_on(2 * k + part)
             if (k, part) == (0, 1):
+                pass_first()
+            if (k, part) == (0, 3):
+                last_first()
+                corner[...] = corner_in[...]
+            pass_on(4 * k + part)
+            if 4 * k + part == ROW_POINT:
                 start_rows()
-                corner[...] = corner_in[...]
 
         for child in range(2):
             finish_block(k, corner.at[child], inv.at[child], factors.at[child])
@@ -354,10 +372,11 @@
         high_low = (jnp.concatenate([one_high, two_high], axis=1), jnp.concatenate([one_low, two_low], axis=1))
         return one, two, high_low
 
+    pass_on(16)
     one, two, _ = solve(own, own_rows[...])
     own_panel[:, : 2 * TILE] = one
     own_panel[:, 2 * TILE :] = two
-    pass_on(8)
+    pass_on(17)
 
     @pl.when(core == 1)
     def _():
@@ -394,31 +413,21 @@
                     for q in range(2):
                         bulk_arrive(child, offset, 1, i, q)
 
-    partner_rows((own, 0), (other, 0))
-
-    @pl.loop(0, 2)
-    def _(group):
+    pairs = (((own, 0), (other, 0)), ((own, -1), (own, 1)), ((other, -1), (other, 1)), ((own, 2), (other, 2)))
+
+    @pl.loop(0, 4)
+    def _(pair):
+        for number in range(4):
+
+            @pl.when(pair == number)
+            def _():
+                pass_on(18 + number)
+                partner_rows(*pairs[number])
+
+        panels(lax.select(pair == 2, other, own), chip_at(lax.select(pair == 0, 0, lax.select(pair == 3, 2, -1))))
+        panels(lax.select(pair == 1, own, other), chip_at(lax.select(pair == 0, 0, lax.select(pair == 3, 2, 1))))
         for part in range(4):
-            factor_panel(4 * group + part, mat.at[0], tile.at[0], upper.at[0], top_inv)
-        panels(lax.select(group == 0, own, other), chip)
-
-    pass_on(9)
-    partner_rows((own, -1), (own, 1))
-
-    @pl.loop(2, 4)
-    def _(group):
-        for part in range(4):
-            factor_panel(4 * group + part, mat.at[0], tile.at[0], upper.at[0], top_inv)
-        panels(own, chip_at(2 * group - 5))
-
-    pass_on(10)
-    partner_rows((other, -1), (other, 1))
-    for offset in (-1, 1):
-        panels(other, chip_at(offset))
-    pass_on(11)
-    partner_rows((own, 2), (other, 2))
-    for child in (own, other):
-        panels(child, chip_at(2))
+            factor_panel(4 * pair + part, mat.at[0], tile.at[0], upper.at[0], top_inv)
 
     def sent(kind):
         for name, make in sends:

time: 81.3 us -> 76 us (0.935)
  the two profiles are of different devices: /device:TPU:65 before, /device:TPU:160 now
where the time goes in v3:
time: 76 us; the launch traced here: 75.9 us
  Pallas kernels  74.4 us (98%)
  between operations  0.81 us (1%)
    pallas_call x1, Pallas kernels, gather_factor(): pl.pallas_call(gather_factor_kernel, out_shape=(jax.ShapeDtypeStruct((row...  65.1 us
    pallas_call x1, Pallas kernels, assemble(): pl.pallas_call(assemble_kernel, out_shape=(jax.ShapeDtypeStruct((rows, 4...  9.34 us

profile of v3, /device:TPU:160, one launch (start us, length us, event | category | flops | bytes accessed | tf_op | source)
XLA Modules:
  0.0 75.9 jit_solution(5815149281835459776)
XLA Ops:
  0.6 65.1 %gather_factor.1 = (f32[256,1536]{1,0:T(8,128)S(1)}, bf16[2,12,128,512]{3,2,1,0:T(8,128)(2,1)S(1)}, bf16[2,12,128,512]{3,2,1,0:T(8,128)(2,1)S(1)}, f32[2,12,128,...) custom-call(f32[256,2048]{1,0:T(8,128)} %bitcast.7, ...), custom_call_target="tpu_custom_call" | custom-call | tf_op jit(solution)/shard_map/gather_factor/pallas_call | solution.py:490
  65.7 0.0 copy-start
  65.7 0.7 copy-done
  66.4 9.3 %assemble.1 = (f32[256,512]{1,0:T(8,128)}, f32[256,128]{1,0:T(8,128)}, f32[256,3968]{1,0:T(8,128)}) custom-call(s32[12,1,32]{2,1,0:T(1,128)S(1)} %bitcast.6, f32[256,2048]{1,0:T(8,128)} %bitcast.8, f32[256,1536]{1,0:T(8,128)S(1)} %get-tuple-element.13.sibling_rows, f32[1,256]{1,0:T(1,128)} %bitcast.10, bf16[2,12,128,512]{3,2,1,0:T(8,128)(2,1)S(1)} %get-tuple-element.14.high, ...), custom_call_target="tpu_custom_call" | custom-call | tf_op jit(solution)/shard_map/assemble/pallas_call | solution.py:649
Async XLA Ops:
  65.7 0.7 copy-start

commit v4 on v3

--- a/solution.py
+++ b/solution.py
@@ -561,20 +561,18 @@
     above = jnp.where((row == 0) & (col == TILE - 1), 1.0, 0.0)
     under = jnp.where((row == TILE - 1) & (col == 0), 1.0, 0.0)
 
-    @pl.loop(0, 32)
-    def _(p):
-        total = jnp.zeros((TILE, TILE), f32)
+    def landed(p):
+        if p == 0:
+            return top[...]
+        total = -above if p == 1 else jnp.zeros((TILE, TILE), f32)
         for child in range(2):
             a = child_of[child, p]
             total = total + jnp.where(a >= 0, column[child, jnp.maximum(a, 0)], 0.0)
-        parent[p] = total
-
-    parent[0] = top[...]
-    parent[1] -= above
+        return total
 
     last = right_stack(*halves(top_inv[...]))
     for q in range(8):
-        block = parent[4 * q : 4 * q + 4].reshape(4 * TILE, TILE)
+        block = jnp.concatenate([landed(p) for p in range(4 * q, 4 * q + 4)], axis=0)
         done = stack_dot(left_stack(*halves(block)), last)
         parent[4 * q : 4 * q + 4] = done.reshape(4, TILE, TILE)
         done_high, done_low = halves(done)
@@ -598,29 +596,35 @@
     for kin in range(2):
         child = half if kin == 0 else 1 - half
         source = own_front if kin == 0 else sib_front
-        for r in range(2):
-            a = child_of[child, place + r]
-            rows = pl.ds(r * TILE, TILE)
-
-            @pl.when(a >= 0)
-            def _():
-                local = 4 * lax.div(a, 3) + lax.rem(a, 3) + 1 - 2 * front_id
-                source_rows = pl.ds(pl.multiple_of(local * TILE, TILE), TILE)
-                lead = left_stack(high[child, a], low[child, a])
-                for g in range(4):
-                    others = right_stack(
-                        high[child, pl.ds(3 * g, 3)].reshape(3 * TILE, 4 * TILE),
-                        low[child, pl.ds(3 * g, 3)].reshape(3 * TILE, 4 * TILE),
-                    )
-                    product = stack_dot(lead, others)
-                    for m in range(3):
-                        b = 3 * g + m
-                        p = index[b, 0, first + child]
-                        t = 4 * g + m + 1 if kin == 0 else b
-                        value = source[source_rows, t * TILE : (t + 1) * TILE] - product[:, m * TILE : (m + 1) * TILE]
-                        if b == 0:
-                            continue
-                        parent_update[rows, columns_of(p)] += value
+        landing = [child_of[child, place + r] for r in range(2)]
+
+        @pl.when((landing[0] >= 0) | (landing[1] >= 0))
+        def _():
+            leads = []
+            source_rows = []
+            for a in landing:
+                tile_row = jnp.maximum(a, 0)
+                leads.append(left_stack(high[child, tile_row], low[child, tile_row]))
+                local = 4 * lax.div(tile_row, 3) + lax.rem(tile_row, 3) + 1 - 2 * front_id
+                local = jnp.where(a >= 0, local, 0)
+                source_rows.append(pl.ds(pl.multiple_of(local * TILE, TILE), TILE))
+            lead = jnp.concatenate(leads, axis=0)
+            for g in range(4):
+                others = right_stack(
+                    high[child, pl.ds(3 * g, 3)].reshape(3 * TILE, 4 * TILE),
+                    low[child, pl.ds(3 * g, 3)].reshape(3 * TILE, 4 * TILE),
+                )
+                product = stack_dot(lead, others)
+                for m in range(3):
+                    b = 3 * g + m
+                    if b == 0:
+                        continue
+                    p = index[b, 0, first + child]
+                    t = 4 * g + m + 1 if kin == 0 else b
+                    for r in range(2):
+                        rows = slice(r * TILE, (r + 1) * TILE)
+                        value = source[source_rows[r], t * TILE : (t + 1) * TILE] - product[rows, m * TILE : (m + 1) * TILE]
+                        parent_update[rows, columns_of(p)] += jnp.where(landing[r] >= 0, value, 0.0)
 
     for r in range(2):
         p = place + r

time: 76 us -> 76.2 us (level)
  no operation moved by 1% of the time
where the time goes in v4:
time: 76.2 us; the launch traced here: 76 us
  Pallas kernels  74.5 us (98%)
  between operations  0.81 us (1%)
    pallas_call x1, Pallas kernels, gather_factor(): pl.pallas_call(gather_factor_kernel, out_shape=(jax.ShapeDtypeStruct((row...  65.1 us
    pallas_call x1, Pallas kernels, assemble(): pl.pallas_call(assemble_kernel, out_shape=(jax.ShapeDtypeStruct((rows, 4...  9.47 us

profile of v4, /device:TPU:160, one launch (start us, length us, event | category | flops | bytes accessed | tf_op | source)
XLA Modules:
  0.0 76.0 jit_solution(5052977454641882918)
XLA Ops:
  0.6 65.1 %gather_factor.1 = (f32[256,1536]{1,0:T(8,128)S(1)}, bf16[2,12,128,512]{3,2,1,0:T(8,128)(2,1)S(1)}, bf16[2,12,128,512]{3,2,1,0:T(8,128)(2,1)S(1)}, f32[2,12,128,...) custom-call(f32[256,2048]{1,0:T(8,128)} %bitcast.7, ...), custom_call_target="tpu_custom_call" | custom-call | tf_op jit(solution)/shard_map/gather_factor/pallas_call | solution.py:490
  65.7 0.0 copy-start
  65.7 0.7 copy-done
  66.4 9.5 %assemble.1 = (f32[256,512]{1,0:T(8,128)}, f32[256,128]{1,0:T(8,128)}, f32[256,3968]{1,0:T(8,128)}) custom-call(s32[12,1,32]{2,1,0:T(1,128)S(1)} %bitcast.6, f32[256,2048]{1,0:T(8,128)} %bitcast.8, f32[256,1536]{1,0:T(8,128)S(1)} %get-tuple-element.13.sibling_rows, f32[1,256]{1,0:T(1,128)} %bitcast.10, bf16[2,12,128,512]{3,2,1,0:T(8,128)(2,1)S(1)} %get-tuple-element.14.high, ...), custom_call_target="tpu_custom_call" | custom-call | tf_op jit(solution)/shard_map/assemble/pallas_call | solution.py:653
Async XLA Ops:
  65.7 0.7 copy-start

commit v5 on v4

--- a/solution.py
+++ b/solution.py
@@ -168,17 +168,18 @@
         stage(front.at[pl.ds(0, TILE), pl.ds(4 * k * TILE, TILE)], corner_slot.at[:, pl.ds(k * TILE, TILE)], core == 0)
     stage_row(0, gathered.at[own, 3 * chip + 1], core == 1)
     stage_row(1, gathered.at[own, 3 * chip + 2 * core])
+
+    stage(weight_row, weights)
+    needed_first = len(staged)
     for k in range(4):
         stage(front.at[:, pl.ds(4 * k * TILE, TILE)], own_rows.at[:, pl.ds(k * TILE, TILE)])
-
-    stage(weight_row, weights)
 
     barrier = pltpu.get_barrier_semaphore()
     greeted = (sibling, right, left, opposite, sibling_right, sibling_left, sibling_opposite, partner)
     for device in greeted:
         pl.semaphore_signal(barrier, inc=1, device_id=device, device_id_type=MESH)
     pl.semaphore_wait(barrier, len(greeted))
-    for condition, copy in staged:
+    for condition, copy in staged[:needed_first]:
         when(condition, copy.wait)
 
     @pl.when((core == 0) & (chip == 0) & (half == 0))
@@ -373,6 +374,8 @@
         return one, two, high_low
 
     pass_on(16)
+    for condition, copy in staged[needed_first:]:
+        when(condition, copy.wait)
     one, two, _ = solve(own, own_rows[...])
     own_panel[:, : 2 * TILE] = one
     own_panel[:, 2 * TILE :] = two

time: 76.2 us -> 76.4 us (level)
  no operation moved by 1% of the time
where the time goes in v5:
time: 76.4 us; the launch traced here: 76.3 us
  Pallas kernels  74.8 us (98%)
  between operations  0.81 us (1%)
    pallas_call x1, Pallas kernels, gather_factor(): pl.pallas_call(gather_factor_kernel, out_shape=(jax.ShapeDtypeStruct((row...  65.3 us
    pallas_call x1, Pallas kernels, assemble(): pl.pallas_call(assemble_kernel, out_shape=(jax.ShapeDtypeStruct((rows, 4...  9.47 us

profile of v5, /device:TPU:160, one launch (start us, length us, event | category | flops | bytes accessed | tf_op | source)
XLA Modules:
  0.0 76.3 jit_solution(13923881237992587973)
XLA Ops:
  0.6 65.3 %gather_factor.1 = (f32[256,1536]{1,0:T(8,128)S(1)}, bf16[2,12,128,512]{3,2,1,0:T(8,128)(2,1)S(1)}, bf16[2,12,128,512]{3,2,1,0:T(8,128)(2,1)S(1)}, f32[2,12,128,...) custom-call(f32[256,2048]{1,0:T(8,128)} %bitcast.7, ...), custom_call_target="tpu_custom_call" | custom-call | tf_op jit(solution)/shard_map/gather_factor/pallas_call | solution.py:493
  66.0 0.0 copy-start
  66.0 0.7 copy-done
  66.6 9.5 %assemble.1 = (f32[256,512]{1,0:T(8,128)}, f32[256,128]{1,0:T(8,128)}, f32[256,3968]{1,0:T(8,128)}) custom-call(s32[12,1,32]{2,1,0:T(1,128)S(1)} %bitcast.6, f32[256,2048]{1,0:T(8,128)} %bitcast.8, f32[256,1536]{1,0:T(8,128)S(1)} %get-tuple-element.13.sibling_rows, f32[1,256]{1,0:T(1,128)} %bitcast.10, bf16[2,12,128,512]{3,2,1,0:T(8,128)(2,1)S(1)} %get-tuple-element.14.high, ...), custom_call_target="tpu_custom_call" | custom-call | tf_op jit(solution)/shard_map/assemble/pallas_call | solution.py:656
Async XLA Ops:
  66.0 0.7 copy-start
